TPU v7x, 32 devices: a whole 2x2x4 slice. The times are simulated.
32 devices in a mesh: tx: 2 (over core), ty: 4 (over y, x), lz: 4 (over z).
Axes of the slice: x: 2, y: 2, z: 4, core: 2. Of those that a mesh axis runs over, the one named last changes fastest.
Arguments:
- test_field: bfloat16 [64, 6, 48, 512], P('tx', None, 'lz', 'ty'), may hold values from -6 to 6
- dir_field: bfloat16 [64, 6, 48, 512], P('tx', None, 'lz', 'ty'), may hold values from -6 to 6
- border_b: bfloat16 [64, 6, 48, 512], P('tx', None, 'lz', 'ty')
- border_c: bfloat16 [64, 6, 48, 512], P('tx', None, 'lz', 'ty')
- land_mask: int32 [64, 512], P('tx', 'ty'), may hold values from 0 to 1, as said below
- active_rows: int32 [64, 4], P('tx', 'ty'), may hold values from -1 to 31, as said below
- cell_blocks: bfloat16 [64, 36, 512], P('tx', None, 'ty'), may hold values from -2.5 to 2.5
- column_k: bfloat16 [288, 288], replicated, may hold values from -0.375 to 0.375
- kappa: float32 [6], replicated, may hold values from 0.2 to 1
Outputs:
- test_image: bfloat16 [64, 6, 48, 512], P('tx', None, 'lz', 'ty')
- dir_image: bfloat16 [64, 6, 48, 512], P('tx', None, 'lz', 'ty')
- border: float32 [3], replicated
Inputs may be any that keep to these rules, and one draw needn't show every extreme that they name: `active_rows`: in each tile the 32 entries name distinct local rows, the active ones, followed by -1 for the rest; some tile has all 32 rows active. `land_mask`: cells whose latitude index y has y % 128 equal to 0 or 127 are ocean.
All inputs are finite; a program needn't handle non-finite values.
Results may differ from a plain program's by a relative error of at most 0.0028.
Values may be sent and summed in bfloat16 or wider, within the bound.
A program may use at most 192 MiB of HBM per device.

v0:
```python
import jax
import jax.numpy as jnp
from jax import lax
from jax.sharding import PartitionSpec as P


def extended(value, sides, width, wrap):
    for axis, dim in sides:
        size, length = (lax.axis_size(axis), value.shape[dim])
        up = [(i, (i + 1) % size) for i in range(size if wrap else size - 1)]
        down = [(j, i) for i, j in up]
        last = lax.slice_in_dim(value, length - width, length, axis=dim)
        initial = lax.slice_in_dim(value, 0, width, axis=dim)
        before = lax.ppermute(last, axis, up)
        after = lax.ppermute(initial, axis, down)
        value = jnp.concatenate([before, value, after], axis=dim)
    return value


def body(
    test_field, dir_field, border_b, border_c, land_mask, active_rows, cell_blocks, column_k, kappa
):
    rows_here, units, layers, cells = test_field.shape
    col_size = column_k.shape[0]
    depth = col_size // units
    lines = jnp.arange(rows_here, dtype=jnp.int32)
    named = jnp.any(active_rows[:, 0][None, :] == lines[:, None], axis=1)
    weight = land_mask.astype(jnp.float32) * named.astype(jnp.float32)[:, None]
    stacked = jnp.concatenate(
        [
            test_field * weight.astype(jnp.bfloat16)[:, None, None, :],
            dir_field * weight.astype(jnp.bfloat16)[:, None, None, :],
        ],
        axis=1,
    )
    column_b = border_b.astype(jnp.float32)
    row_c = border_c.astype(jnp.float32)
    norm_b = jnp.sum(column_b * column_b)
    norm_c = jnp.sum(row_c * row_c)
    value_c = jnp.sum(row_c * test_field.astype(jnp.float32))
    part = lax.all_to_all(stacked, "lz", split_axis=0, concat_axis=2, tiled=True)
    group = part.shape[0]
    span = part.shape[3]
    flat = part.reshape(group, 2, col_size, span)
    product = jnp.einsum("pq,gfqc->gfpc", column_k, flat, preferred_element_type=jnp.float32)
    product = product.astype(jnp.bfloat16).reshape(group, 2 * units, depth, span)
    coupled = lax.all_to_all(product, "lz", split_axis=2, concat_axis=0, tiled=True).astype(
        jnp.float32
    )
    lon_padded = extended(stacked, (("tx", 0),), 1, True)
    lat_padded = extended(stacked, (("ty", 3),), 1, False)
    center = stacked.astype(jnp.float32)
    spread = (
        lon_padded[2:].astype(jnp.float32)
        + lon_padded[:-2].astype(jnp.float32)
        + lat_padded[..., 2:].astype(jnp.float32)
        + lat_padded[..., :-2].astype(jnp.float32)
        - 4.0 * center
    )
    rates = jnp.concatenate([kappa, kappa]).reshape(1, 2 * units, 1, 1)
    blocks = cell_blocks.reshape(rows_here, units, units, cells)
    local = jnp.einsum(
        "xuwy,xfwzy->xfuzy",
        blocks,
        stacked.reshape(rows_here, 2, units, layers, cells),
        preferred_element_type=jnp.float32,
    ).reshape(rows_here, 2 * units, layers, cells)
    image = weight[:, None, None, :] * (coupled + local + rates * spread)
    test_full = image[:, :units]
    dir_full = image[:, units:]
    value_a = jnp.sum(column_b * test_full)
    value_e = jnp.sum(column_b * dir_full)
    norm_b, norm_c, value_c, value_a, value_e = lax.psum(
        (norm_b, norm_c, value_c, value_a, value_e), ("tx", "ty", "lz")
    )
    border = jnp.stack(
        [value_a / jnp.sqrt(norm_b), value_e / jnp.sqrt(norm_b), value_c / jnp.sqrt(norm_c)]
    )
    return (test_full.astype(jnp.bfloat16), dir_full.astype(jnp.bfloat16), border)


def solution(mesh):
    in_specs = (
        P("tx", None, "lz", "ty"),
        P("tx", None, "lz", "ty"),
        P("tx", None, "lz", "ty"),
        P("tx", None, "lz", "ty"),
        P("tx", "ty"),
        P("tx", "ty"),
        P("tx", None, "ty"),
        P(),
        P(),
    )
    out_specs = (P("tx", None, "lz", "ty"), P("tx", None, "lz", "ty"), P())
    return jax.shard_map(body, mesh=mesh, in_specs=in_specs, out_specs=out_specs, check_vma=False)
```

profile of v0, /device:TPU:0, one launch (start us, length us, event | category | flops | bytes accessed | tf_op | source)
XLA Modules:
  0.0 150.9 jit_solution(9420423562500274029)
XLA Ops:
  0.6 0.0 copy-start
  0.6 0.8 fusion.13
  1.5 0.8 fusion.14
  2.3 1.3 broadcast_multiply_fusion.1
  3.6 0.1 pad_maximum_fusion
  3.7 1.7 %copy.43 = bf16[32,12,12,128]{3,2,1,0:T(8,128)(2,1)} copy(bf16[32,12,12,128]{3,0,2,1:T(8,128)(2,1)S(1)} %pad_maximum_fusion) | data formatting | bytes 2359296 | tf_op jit(solution)/shard_map/concatenate | solution.py:29
  5.4 6.3 %all-to-all-start = ((bf16[32,12,12,128]{3,2,1,0:T(8,128)(2,1)}), bf16[32,12,12,128]{3,2,1,0:T(8,128)(2,1)}, u32[]{:S(2)}, u32[]{:S(2)}) async-start(bf16[32,12,12,128]{3,2,1,0:T(8,128)(2,1)} %copy.43), calls=%async_computation | async-start | bytes 3145728 | tf_op jit(solution)/shard_map/all_to_all | solution.py:41
  11.7 1.9 %fusion.7 = (bf16[32,12,12,1]{3,0,2,1:T(8,128)(2,1)}, bf16[32,12,12,1]{3,0,2,1:T(8,128)(2,1)}) fusion(bf16[32,6,12,128]{3,0,2,1:T(8,128)(2,1)S(1)} %get-tuple-element.21, bf16[32,6,12,128]{3,0,2,1:T(8,128)(2,1)S(1)} %get-tuple-element.22), kind=kLoop, calls=%fused_computation.25 | loop fusion | flops 9216 | bytes 1198080 | tf_op jit(solution)/shard_map/concatenate | solution.py:29
  13.6 2.4 %copy.53 = bf16[32,12,12,1]{0,2,3,1:T(8,128)(2,1)S(1)} copy(bf16[32,12,12,1]{3,0,2,1:T(8,128)(2,1)} %get-tuple-element.19) | data formatting | bytes 18432 | tf_op jit(solution)/shard_map/slice | solution.py:13
  16.0 1.3 collective-permute-start.2
  17.3 2.5 %copy.55 = bf16[32,12,12,1]{0,2,3,1:T(8,128)(2,1)S(1)} copy(bf16[32,12,12,1]{3,0,2,1:T(8,128)(2,1)} %get-tuple-element.20) | data formatting | bytes 18432 | tf_op jit(solution)/shard_map/slice | solution.py:12
  19.8 4.6 %collective-permute-start.3 = (bf16[32,12,12,1]{0,2,3,1:T(8,128)(2,1)S(1)}, bf16[32,12,12,1]{0,2,3,1:T(8,128)(2,1)S(1)}, u32[]{:S(2)}, u32[]{:S(2)}) collective-permute-start(bf16[32,12,12,1]{0,2,3,1:T(8,128)(2,1)S(1)} %copy.55), channel_id=1, source_target_pairs={{0,4},{4,8},{8,12},{1,5},{5,9},{9,13},{2,6},{6,10},{10,14},{3,7},{... | collective-permute-start | bytes 27656 | tf_op jit(solution)/shard_map/ppermute | solution.py:14
  24.4 0.2 fusion.11
  24.5 0.1 collective-permute-start
  24.6 0.5 collective-permute-start.1
  25.1 10.2 %copy.50 = bf16[32,2,6,12,128]{3,2,1,4,0:T(8,128)(2,1)} copy(bf16[32,2,6,12,128]{4,0,3,2,1:T(8,128)(2,1)S(1)} %bitcast.37) | data formatting | bytes 2359296 | tf_op jit(solution)/shard_map/reshape | solution.py:65
  35.3 0.0 copy-done.6
  35.3 5.5 %copy.58 = bf16[32,6,6,128,1]{2,1,4,3,0:T(8,128)(2,1)} copy(bf16[32,6,6,128,1]{3,0,2,1,4:T(8,128)(2,1)S(1)} %bitcast.41) | data formatting | bytes 589824 | tf_op jit(solution)/shard_map/reshape | solution.py:61
  40.8 0.0 copy-done.3
  40.8 0.0 copy-done.4
  40.8 1.0 fusion.3
  41.8 7.0 %all-to-all-done = bf16[32,12,12,128]{3,2,1,0:T(8,128)(2,1)} async-done(((bf16[32,12,12,128]{3,2,1,0:T(8,128)(2,1)}), bf16[32,12,12,128]{3,2,1,0:T(8,128)(2,1)}, u32[]{:S(2)}, u32[]{:S(2)}) %all-to-all-start) | async-done | bytes 1179680 | tf_op jit(solution)/shard_map/all_to_all | solution.py:41
  48.8 2.8 %copy.45 = bf16[8,12,4,12,128]{4,0,3,2,1:T(8,128)(2,1)S(1)} copy(bf16[8,12,4,12,128]{4,3,1,0,2:T(8,128)(2,1)} %bitcast.3) | data formatting | bytes 2359296 | tf_op jit(solution)/shard_map/all_to_all | solution.py:41
  51.6 0.0 copy-done
  51.6 0.8 convolution_convert_fusion
  52.4 1.9 %copy.47 = bf16[8,12,48,128]{3,0,1,2:T(8,128)(2,1)} copy(bf16[8,12,48,128]{3,2,1,0:T(8,128)(2,1)S(1)} %bitcast.39) | data formatting | bytes 2359296 | tf_op jit(solution)/shard_map/reshape | solution.py:46
  54.2 4.5 %all-to-all-start.1 = ((bf16[8,12,48,128]{3,0,1,2:T(8,128)(2,1)}), bf16[8,12,48,128]{3,0,1,2:T(8,128)(2,1)}, u32[]{:S(2)}, u32[]{:S(2)}) async-start(bf16[8,12,48,128]{3,0,1,2:T(8,128)(2,1)} %copy.47), calls=%async_computation.1 | async-start | bytes 2359296 | tf_op jit(solution)/shard_map/all_to_all | solution.py:47
  58.7 0.0 copy-start.7
  58.7 20.0 %convolution_bitcast_fusion = f32[32,2,6,12,128]{3,2,1,4,0:T(8,128)} fusion(bf16[32,2,6,12,128]{3,2,1,4,0:T(8,128)(2,1)} %copy.50, bf16[32,6,6,128,1]{2,1,4,3,0:T(8,128)(2,1)} %copy.58), kind=kOutput, calls=%fused_computation | convolution fusion | flops 7077888 | bytes 3833856 | tf_op jit(solution)/shard_map/xuwy,xfwzy->xfuzy/dot_general | solution.py:62
  78.7 0.0 copy-done.7
  78.7 0.1 pad_maximum_fusion.9
  78.8 15.6 %copy.52 = f32[32,2,6,12,128]{4,0,3,2,1:T(8,128)} copy(f32[32,2,6,12,128]{3,2,1,4,0:T(8,128)} %convolution_bitcast_fusion) | data formatting | bytes 4718592 | tf_op jit(solution)/shard_map/xuwy,xfwzy->xfuzy/transpose | solution.py:62
  94.4 0.0 collective-permute-done.2
  94.4 1.0 copy.54
  95.4 0.0 collective-permute-done.3
  95.4 1.9 %copy.56 = bf16[32,12,12,1]{3,0,2,1:T(8,128)(2,1)} copy(bf16[32,12,12,1]{0,2,3,1:T(8,128)(2,1)S(1)} %collective-permute-done.3) | data formatting | bytes 18432 | tf_op jit(solution)/shard_map/ppermute | solution.py:14
  97.3 0.0 all-to-all-done.1
  97.3 1.6 %copy.48 = bf16[8,12,48,128]{3,0,2,1:T(8,128)(2,1)S(1)} copy(bf16[8,12,48,128]{3,0,1,2:T(8,128)(2,1)} %all-to-all-done.1) | data formatting | bytes 2359296 | tf_op jit(solution)/shard_map/all_to_all | solution.py:47
  99.0 0.0 collective-permute-done
  99.0 0.0 collective-permute-done.1
  99.0 0.0 copy-done.2
  99.0 4.8 %fusion.1 = f32[32,12,12,128]{3,0,2,1:T(8,128)S(1)} fusion(f32[32,2,6,12,128]{4,0,3,2,1:T(8,128)} %copy.52, bf16[32,12,12,1]{3,0,2,1:T(8,128)(2,1)S(1)} %copy-done.2, bf16[32,6,12,128]{3,0,2,1:T(8,128)(2,1)S(1)} %get-tuple-element.22, bf16[32,6,12,128]{3,0,2,1:T(8,128)(2,1)S(1)} %get-tuple-element.21, bf16[32,12,12,1]{3,0,2,1:T(8,128)(2,1)S(1)} %copy.54, ...), kind=kLoop, calls=%fused_computation.4 | loop fusion | flops 22413312 | bytes 7186480 | tf_op jit(solution)/shard_map/mul | solution.py:68
  103.8 0.0 copy-start.5
  103.8 0.0 copy-start.1
  103.8 1.3 fusion.15
  105.1 1.1 fusion.4
  106.2 40.9 %all-reduce = (f32[]{:T(128)}, f32[]{:T(128)}, f32[]{:T(128)}, f32[]{:T(128)}, f32[]{:T(128)}) all-reduce(f32[]{:T(128)} %get-tuple-element.7, f32[]{:T(128)} %get-tuple-element.6, f32[]{:T(128)} %get-tuple-element.4, f32[]{:T(128)} %get-tuple-element.5, f32[]{:T(128)} %get-tuple-element.3), channel_id=1, replica_groups=mesh['tx'=2,'ty'=4,'lz'=4] {'tx','ty','lz'}, use_global_device_ids=true, to_apply=%region_8.0 | all-reduce | flops 5 | bytes 40 | tf_op jit(solution)/shard_map/psum | solution.py:73
  150.3 0.6 pad_maximum_fusion.10
  (7 shorter events, 0.0 us)
Async XLA Ops:
  0.6 50.9 %copy-start = (bf16[288,288]{1,0:T(8,128)(2,1)S(1)}, bf16[288,288]{1,0:T(8,128)(2,1)}, u32[]{:S(2)}) copy-start(bf16[288,288]{1,0:T(8,128)(2,1)} %param.16) | copy-start | bytes 497668
  5.4 43.4 %all-to-all-start = ((bf16[32,12,12,128]{3,2,1,0:T(8,128)(2,1)}), bf16[32,12,12,128]{3,2,1,0:T(8,128)(2,1)}, u32[]{:S(2)}, u32[]{:S(2)}) async-start(bf16[32,12,12,128]{3,2,1,0:T(8,128)(2,1)} %copy.43), calls=%async_computation | async-start | bytes 3145728 | tf_op jit(solution)/shard_map/all_to_all | solution.py:41
  16.0 78.4 %collective-permute-start.2 = (bf16[32,12,12,1]{0,2,3,1:T(8,128)(2,1)S(1)}, bf16[32,12,12,1]{0,2,3,1:T(8,128)(2,1)S(1)}, u32[]{:S(2)}, u32[]{:S(2)}) collective-permute-start(bf16[32,12,12,1]{0,2,3,1:T(8,128)(2,1)S(1)} %copy.53), channel_id=1, source_target_pairs={{4,0},{8,4},{12,8},{5,1},{9,5},{13,9},{6,2},{10,6},{14,10},{7,3},{... | collective-permute-start | bytes 27656 | tf_op jit(solution)/shard_map/ppermute | solution.py:15
  19.8 75.6 %collective-permute-start.3 = (bf16[32,12,12,1]{0,2,3,1:T(8,128)(2,1)S(1)}, bf16[32,12,12,1]{0,2,3,1:T(8,128)(2,1)S(1)}, u32[]{:S(2)}, u32[]{:S(2)}) collective-permute-start(bf16[32,12,12,1]{0,2,3,1:T(8,128)(2,1)S(1)} %copy.55), channel_id=1, source_target_pairs={{0,4},{4,8},{8,12},{1,5},{5,9},{9,13},{2,6},{6,10},{10,14},{3,7},{... | collective-permute-start | bytes 27656 | tf_op jit(solution)/shard_map/ppermute | solution.py:14
  24.5 74.5 %collective-permute-start = (bf16[1,12,12,128]{3,0,2,1:T(2,128)(2,1)S(1)}, bf16[1,12,12,128]{3,0,2,1:T(2,128)(2,1)S(1)}, u32[]{:S(2)}, u32[]{:S(2)}) collective-permute-start(bf16[1,12,12,128]{3,0,2,1:T(2,128)(2,1)S(1)} %get-tuple-element.17), channel_id=1, source_target_pairs={{16,0},{0,16},{17,1},{1,17},{18,2},{2,18},{19,3},{3,19},{20,4},{4,... | collective-permute-start | bytes 110600 | tf_op jit(solution)/shard_map/ppermute | solution.py:15
  24.6 74.4 %collective-permute-start.1 = (bf16[1,12,12,128]{3,0,2,1:T(2,128)(2,1)S(1)}, bf16[1,12,12,128]{3,0,2,1:T(2,128)(2,1)S(1)}, u32[]{:S(2)}, u32[]{:S(2)}) collective-permute-start(bf16[1,12,12,128]{3,0,2,1:T(2,128)(2,1)S(1)} %get-tuple-element.18), channel_id=1, source_target_pairs={{0,16},{16,0},{1,17},{17,1},{2,18},{18,2},{3,19},{19,3},{4,20},{20... | collective-permute-start | bytes 110600 | tf_op jit(solution)/shard_map/ppermute | solution.py:14
  25.1 10.2 %copy-start.6 = (bf16[32,36,128]{2,0,1:T(8,128)(2,1)S(1)}, bf16[32,36,128]{2,0,1:T(8,128)(2,1)}, u32[]{:S(2)}) copy-start(bf16[32,36,128]{2,0,1:T(8,128)(2,1)} %param.15) | copy-start | bytes 884740
  35.3 5.5 %copy-start.3 = (bf16[32,6,12,128]{3,0,2,1:T(8,128)(2,1)S(1)}, bf16[32,6,12,128]{3,0,2,1:T(8,128)(2,1)}, u32[]{:S(2)}) copy-start(bf16[32,6,12,128]{3,0,2,1:T(8,128)(2,1)} %param.9) | copy-start | bytes 1769476
  35.3 5.5 %copy-start.4 = (bf16[32,6,12,128]{3,0,2,1:T(8,128)(2,1)S(1)}, bf16[32,6,12,128]{3,0,2,1:T(8,128)(2,1)}, u32[]{:S(2)}) copy-start(bf16[32,6,12,128]{3,0,2,1:T(8,128)(2,1)} %param.12) | copy-start | bytes 1769476
  54.2 43.1 %all-to-all-start.1 = ((bf16[8,12,48,128]{3,0,1,2:T(8,128)(2,1)}), bf16[8,12,48,128]{3,0,1,2:T(8,128)(2,1)}, u32[]{:S(2)}, u32[]{:S(2)}) async-start(bf16[8,12,48,128]{3,0,1,2:T(8,128)(2,1)} %copy.47), calls=%async_computation.1 | async-start | bytes 2359296 | tf_op jit(solution)/shard_map/all_to_all | solution.py:47
  58.7 20.0 %copy-start.7 = (f32[6]{0:T(128)S(1)}, f32[6]{0:T(128)}, u32[]{:S(2)}) copy-start(f32[6]{0:T(128)} %param.17) | copy-start | bytes 76
  97.3 1.7 %copy-start.2 = (bf16[32,12,12,1]{3,0,2,1:T(8,128)(2,1)S(1)}, bf16[32,12,12,1]{3,0,2,1:T(8,128)(2,1)}, u32[]{:S(2)}) copy-start(bf16[32,12,12,1]{3,0,2,1:T(8,128)(2,1)} %copy.56) | copy-start | bytes 27652
  103.8 1.3 copy-start.5
  103.8 47.1 %copy-start.1 = (bf16[288,288]{1,0:T(8,128)(2,1)S(1)}, bf16[288,288]{1,0:T(8,128)(2,1)}, u32[]{:S(2)}) copy-start(bf16[288,288]{1,0:T(8,128)(2,1)} %param.16) | copy-start | bytes 497668
where the time goes:
time: 152 us; the launch traced here: 151 us
  local copies, waits for them, and re-layouts  48.4 us (32%)
  blocking collectives  40.9 us (27%)
  matrix products  20.8 us (14%)
  starting transfers between devices  17.2 us (11%)
  other arithmetic  12.6 us (8%)
  waiting for transfers between devices  7.02 us (5%)
  between operations  3.94 us (3%)
    psum x1, blocking collectives, body(): lax.psum((norm_b, norm_c, value_c, value_a, value_e), ('tx', 'ty', 'lz'))  40.9 us
    dot_general x1, matrix products, body(): jnp.einsum('xuwy,xfwzy->xfuzy', blocks, stacked.reshape(rows_here, 2, uni...  20 us
    transpose x1, local copies, waits for them, and re-layouts, body(): jnp.einsum('xuwy,xfwzy->xfuzy', blocks, stacked.reshape(rows_here, 2, uni...  15.6 us
    reshape x1, local copies, waits for them, and re-layouts, body(): stacked.reshape(rows_here, 2, units, layers, cells)  10.2 us
    all_to_all x1, waiting for transfers between devices, body(): lax.all_to_all(stacked, 'lz', split_axis=0, concat_axis=2, tiled=True)  7.01 us
    all_to_all x1, starting transfers between devices, body(): lax.all_to_all(stacked, 'lz', split_axis=0, concat_axis=2, tiled=True)  6.35 us
    reshape x1, local copies, waits for them, and re-layouts, body(): blocks = cell_blocks.reshape(rows_here, units, units, cells)  5.47 us
    ppermute x2, starting transfers between devices, extended(): before = lax.ppermute(last, axis, up)  5.05 us
  transfers between devices with their start and end apart: 6, of which 1 were waited for; matrix products, arithmetic and copies ran while one was open for 46% of the time, Pallas kernels for 0%

commit v1 on v0

--- a/solution.py
+++ b/solution.py
@@ -38,7 +38,10 @@
     norm_b = jnp.sum(column_b * column_b)
     norm_c = jnp.sum(row_c * row_c)
     value_c = jnp.sum(row_c * test_field.astype(jnp.float32))
-    part = lax.all_to_all(stacked, "lz", split_axis=0, concat_axis=2, tiled=True)
+    part = jnp.concatenate(
+        lax.all_to_all(jnp.stack(jnp.split(stacked, lax.axis_size("lz"), axis=0)), "lz", 0, 0),
+        axis=2,
+    )
     group = part.shape[0]
     span = part.shape[3]
     flat = part.reshape(group, 2, col_size, span)

time: 152 us -> 142 us (0.934)
  waiting for transfers between devices: 7.02 us -> 1.34 us
  local copies, waits for them, and re-layouts: 48.4 us -> 44.4 us
    all_to_all x1, waiting for transfers between devices: 7.01 us -> 1.33 us  [body(): lax.all_to_all(jnp.stack(jnp.split(stacked, lax.axis_size('lz'), axis=0))...]
    concatenate x1 -> x0, local copies, waits for them, and re-layouts: 1.67 us -> none  [body(): jnp.concatenate([test_field * weight.astype(jnp.bfloat16)[:, None, None,...]
    ppermute x2, starting transfers between devices: 5.05 us -> 3.47 us  [extended(): before = lax.ppermute(last, axis, up)]
  transfers between devices with their start and end apart: 6 -> 6, of which waited for: 1 -> 1; matrix products, arithmetic and copies ran while one was open for 46% -> 47% of each run, Pallas kernels for 0% -> 0%
where the time goes in v1:
time: 142 us
  local copies, waits for them, and re-layouts  44.4 us (31%)
  blocking collectives  41.6 us (29%)
  matrix products  20.8 us (15%)
  starting transfers between devices  16.1 us (11%)
  other arithmetic  13.3 us (9%)
  between operations  4.04 us (3%)
    psum x1, blocking collectives, body(): lax.psum((norm_b, norm_c, value_c, value_a, value_e), ('tx', 'ty', 'lz'))  41.6 us
    dot_general x1, matrix products, body(): jnp.einsum('xuwy,xfwzy->xfuzy', blocks, stacked.reshape(rows_here, 2, uni...  20 us
    transpose x1, local copies, waits for them, and re-layouts, body(): jnp.einsum('xuwy,xfwzy->xfuzy', blocks, stacked.reshape(rows_here, 2, uni...  15.7 us
    reshape x1, local copies, waits for them, and re-layouts, body(): stacked.reshape(rows_here, 2, units, layers, cells)  10.2 us
    all_to_all x1, starting transfers between devices, body(): lax.all_to_all(jnp.stack(jnp.split(stacked, lax.axis_size('lz'), axis=0))...  6.35 us
    reshape x1, local copies, waits for them, and re-layouts, body(): blocks = cell_blocks.reshape(rows_here, units, units, cells)  5.48 us
    mul x1, other arithmetic, body(): image = weight[:, None, None, :] * (coupled + local + rates * spread)  4.71 us
    all_to_all x1, starting transfers between devices, body(): lax.all_to_all(product, 'lz', split_axis=2, concat_axis=0, tiled=True)  4.47 us
  transfers between devices with their start and end apart: 6, of which 1 were waited for; matrix products, arithmetic and copies ran while one was open for 47% of the time, Pallas kernels for 0%

profile of v1, /device:TPU:0, one launch (start us, length us, event | category | flops | bytes accessed | tf_op | source)
XLA Modules:
  0.0 141.6 jit_solution(2436970044934268014)
XLA Ops:
  0.6 0.0 copy-start
  0.6 0.8 fusion.21
  1.5 0.8 fusion.22
  2.3 1.3 broadcast_multiply_fusion.1
  3.6 0.1 fusion.11
  3.7 1.2 pad_maximum_fusion.9
  4.9 6.3 %all-to-all-start = ((bf16[4,8,12,12,128]{4,1,3,2,0:T(8,128)(2,1)}), bf16[4,8,12,12,128]{4,1,3,2,0:T(8,128)(2,1)}, u32[]{:S(2)}, u32[]{:S(2)}) async-start(bf16[4,8,12,12,128]{4,1,3,2,0:T(8,128)(2,1)} %pad_maximum_fusion.9), calls=%async_computation | async-start | bytes 2359296 | tf_op jit(solution)/shard_map/all_to_all | solution.py:42
  11.3 1.5 %fusion.7 = (bf16[32,12,12,1]{3,0,2,1:T(8,128)(2,1)S(1)}, bf16[32,12,12,1]{3,0,2,1:T(8,128)(2,1)}) fusion(bf16[32,6,12,128]{3,0,2,1:T(8,128)(2,1)S(1)} %get-tuple-element.25, bf16[32,6,12,128]{3,0,2,1:T(8,128)(2,1)S(1)} %get-tuple-element.26), kind=kLoop, calls=%fused_computation.33 | loop fusion | flops 9216 | bytes 1198080 | tf_op jit(solution)/shard_map/concatenate | solution.py:29
  12.7 2.4 %copy.59 = bf16[32,12,12,1]{0,2,3,1:T(8,128)(2,1)S(1)} copy(bf16[32,12,12,1]{3,0,2,1:T(8,128)(2,1)} %get-tuple-element.20) | data formatting | bytes 18432 | tf_op jit(solution)/shard_map/slice | solution.py:12
  15.2 3.4 %collective-permute-start.3 = (bf16[32,12,12,1]{0,2,3,1:T(8,128)(2,1)S(1)}, bf16[32,12,12,1]{0,2,3,1:T(8,128)(2,1)S(1)}, u32[]{:S(2)}, u32[]{:S(2)}) collective-permute-start(bf16[32,12,12,1]{0,2,3,1:T(8,128)(2,1)S(1)} %copy.59), channel_id=1, source_target_pairs={{0,4},{4,8},{8,12},{1,5},{5,9},{9,13},{2,6},{6,10},{10,14},{3,7},{... | collective-permute-start | bytes 27656 | tf_op jit(solution)/shard_map/ppermute | solution.py:14
  18.6 1.2 copy.57
  19.8 1.3 collective-permute-start.2
  21.1 0.2 fusion.19
  21.3 0.1 collective-permute-start.1
  21.4 0.5 collective-permute-start
  21.9 0.1 pad_maximum_fusion
  22.0 0.0 copy-start.6
  22.0 10.2 %copy.54 = bf16[32,2,6,12,128]{3,2,1,4,0:T(8,128)(2,1)} copy(bf16[32,2,6,12,128]{4,0,3,2,1:T(8,128)(2,1)S(1)} %bitcast.45) | data formatting | bytes 2359296 | tf_op jit(solution)/shard_map/reshape | solution.py:68
  32.2 0.0 copy-done.6
  32.2 5.5 %copy.62 = bf16[32,6,6,128,1]{2,1,4,3,0:T(8,128)(2,1)} copy(bf16[32,6,6,128,1]{3,0,2,1,4:T(8,128)(2,1)S(1)} %bitcast.48) | data formatting | bytes 589824 | tf_op jit(solution)/shard_map/reshape | solution.py:64
  37.7 0.0 copy-done.3
  37.7 0.9 fusion.3
  38.6 1.3 all-to-all-done
  39.9 1.4 copy.49
  41.3 0.8 convolution_convert_fusion
  42.1 1.9 %copy.51 = bf16[8,12,48,128]{3,0,1,2:T(8,128)(2,1)} copy(bf16[8,12,48,128]{3,2,1,0:T(8,128)(2,1)S(1)} %bitcast.47) | data formatting | bytes 2359296 | tf_op jit(solution)/shard_map/reshape | solution.py:49
  43.9 4.5 %all-to-all-start.1 = ((bf16[8,12,48,128]{3,0,1,2:T(8,128)(2,1)}), bf16[8,12,48,128]{3,0,1,2:T(8,128)(2,1)}, u32[]{:S(2)}, u32[]{:S(2)}) async-start(bf16[8,12,48,128]{3,0,1,2:T(8,128)(2,1)} %copy.51), calls=%async_computation.1 | async-start | bytes 2359296 | tf_op jit(solution)/shard_map/all_to_all | solution.py:50
  48.4 0.0 copy-start.7
  48.4 20.0 %convolution_bitcast_fusion = f32[32,2,6,12,128]{3,2,1,4,0:T(8,128)} fusion(bf16[32,2,6,12,128]{3,2,1,4,0:T(8,128)(2,1)} %copy.54, bf16[32,6,6,128,1]{2,1,4,3,0:T(8,128)(2,1)} %copy.62), kind=kOutput, calls=%fused_computation | convolution fusion | flops 7077888 | bytes 3833856 | tf_op jit(solution)/shard_map/xuwy,xfwzy->xfuzy/dot_general | solution.py:65
  68.4 0.1 pad_maximum_fusion.10
  68.5 15.7 %copy.56 = f32[32,2,6,12,128]{4,0,3,2,1:T(8,128)} copy(f32[32,2,6,12,128]{3,2,1,4,0:T(8,128)} %convolution_bitcast_fusion) | data formatting | bytes 4718592 | tf_op jit(solution)/shard_map/xuwy,xfwzy->xfuzy/transpose | solution.py:65
  84.1 0.0 collective-permute-done.3
  84.1 1.0 copy.60
  85.1 0.0 collective-permute-done.2
  85.1 1.9 %copy.58 = bf16[32,12,12,1]{3,0,2,1:T(8,128)(2,1)} copy(bf16[32,12,12,1]{0,2,3,1:T(8,128)(2,1)S(1)} %collective-permute-done.2) | data formatting | bytes 18432 | tf_op jit(solution)/shard_map/ppermute | solution.py:15
  87.1 0.0 all-to-all-done.1
  87.1 1.7 %copy.52 = bf16[8,12,48,128]{3,0,2,1:T(8,128)(2,1)S(1)} copy(bf16[8,12,48,128]{3,0,1,2:T(8,128)(2,1)} %all-to-all-done.1) | data formatting | bytes 2359296 | tf_op jit(solution)/shard_map/all_to_all | solution.py:50
  88.8 0.0 collective-permute-done.1
  88.8 0.0 collective-permute-done
  88.8 0.3 copy-done.2
  89.1 4.7 %fusion.1 = f32[32,12,12,128]{3,0,2,1:T(8,128)S(1)} fusion(f32[32,2,6,12,128]{4,0,3,2,1:T(8,128)S(1)} %copy-done.2, bf16[32,12,12,1]{3,0,2,1:T(8,128)(2,1)S(1)} %copy.60, bf16[32,6,12,128]{3,0,2,1:T(8,128)(2,1)S(1)} %get-tuple-element.26, bf16[32,6,12,128]{3,0,2,1:T(8,128)(2,1)S(1)} %get-tuple-element.25, bf16[32,12,12,1]{3,0,2,1:T(8,128)(2,1)} %copy.58, ...), kind=kLoop, calls=%fused_computation.21 | loop fusion | flops 22413312 | bytes 7186480 | tf_op jit(solution)/shard_map/mul | solution.py:71
  93.8 0.0 copy-start.5
  93.8 0.0 copy-start.1
  93.8 1.3 fusion.23
  95.1 0.0 copy-done.5
  95.1 1.1 fusion.4
  96.2 41.6 %all-reduce = (f32[]{:T(128)}, f32[]{:T(128)}, f32[]{:T(128)}, f32[]{:T(128)}, f32[]{:T(128)}) all-reduce(f32[]{:T(128)} %get-tuple-element.7, f32[]{:T(128)} %get-tuple-element.6, f32[]{:T(128)} %get-tuple-element.4, f32[]{:T(128)} %get-tuple-element.5, f32[]{:T(128)} %get-tuple-element.3), channel_id=1, replica_groups=mesh['tx'=2,'ty'=4,'lz'=4] {'tx','ty','lz'}, use_global_device_ids=true, to_apply=%region_8.0 | all-reduce | flops 5 | bytes 40 | tf_op jit(solution)/shard_map/psum | solution.py:76
  141.0 0.6 pad_maximum_fusion.11
  (8 shorter events, 0.0 us)
Async XLA Ops:
  0.6 40.7 %copy-start = (bf16[288,288]{1,0:T(8,128)(2,1)S(1)}, bf16[288,288]{1,0:T(8,128)(2,1)}, u32[]{:S(2)}) copy-start(bf16[288,288]{1,0:T(8,128)(2,1)} %param.16) | copy-start | bytes 497668
  4.9 35.0 %all-to-all-start = ((bf16[4,8,12,12,128]{4,1,3,2,0:T(8,128)(2,1)}), bf16[4,8,12,12,128]{4,1,3,2,0:T(8,128)(2,1)}, u32[]{:S(2)}, u32[]{:S(2)}) async-start(bf16[4,8,12,12,128]{4,1,3,2,0:T(8,128)(2,1)} %pad_maximum_fusion.9), calls=%async_computation | async-start | bytes 2359296 | tf_op jit(solution)/shard_map/all_to_all | solution.py:42
  15.2 69.0 %collective-permute-start.3 = (bf16[32,12,12,1]{0,2,3,1:T(8,128)(2,1)S(1)}, bf16[32,12,12,1]{0,2,3,1:T(8,128)(2,1)S(1)}, u32[]{:S(2)}, u32[]{:S(2)}) collective-permute-start(bf16[32,12,12,1]{0,2,3,1:T(8,128)(2,1)S(1)} %copy.59), channel_id=1, source_target_pairs={{0,4},{4,8},{8,12},{1,5},{5,9},{9,13},{2,6},{6,10},{10,14},{3,7},{... | collective-permute-start | bytes 27656 | tf_op jit(solution)/shard_map/ppermute | solution.py:14
  19.8 65.3 %collective-permute-start.2 = (bf16[32,12,12,1]{0,2,3,1:T(8,128)(2,1)S(1)}, bf16[32,12,12,1]{0,2,3,1:T(8,128)(2,1)S(1)}, u32[]{:S(2)}, u32[]{:S(2)}) collective-permute-start(bf16[32,12,12,1]{0,2,3,1:T(8,128)(2,1)S(1)} %copy.57), channel_id=1, source_target_pairs={{4,0},{8,4},{12,8},{5,1},{9,5},{13,9},{6,2},{10,6},{14,10},{7,3},{... | collective-permute-start | bytes 27656 | tf_op jit(solution)/shard_map/ppermute | solution.py:15
  21.3 67.5 %collective-permute-start.1 = (bf16[1,12,12,128]{3,0,2,1:T(2,128)(2,1)S(1)}, bf16[1,12,12,128]{3,0,2,1:T(2,128)(2,1)S(1)}, u32[]{:S(2)}, u32[]{:S(2)}) collective-permute-start(bf16[1,12,12,128]{3,0,2,1:T(2,128)(2,1)S(1)} %get-tuple-element.18), channel_id=1, source_target_pairs={{0,16},{16,0},{1,17},{17,1},{2,18},{18,2},{3,19},{19,3},{4,20},{20... | collective-permute-start | bytes 110600 | tf_op jit(solution)/shard_map/ppermute | solution.py:14
  21.4 67.4 %collective-permute-start = (bf16[1,12,12,128]{3,0,2,1:T(2,128)(2,1)S(1)}, bf16[1,12,12,128]{3,0,2,1:T(2,128)(2,1)S(1)}, u32[]{:S(2)}, u32[]{:S(2)}) collective-permute-start(bf16[1,12,12,128]{3,0,2,1:T(2,128)(2,1)S(1)} %get-tuple-element.17), channel_id=1, source_target_pairs={{16,0},{0,16},{17,1},{1,17},{18,2},{2,18},{19,3},{3,19},{20,4},{4,... | collective-permute-start | bytes 110600 | tf_op jit(solution)/shard_map/ppermute | solution.py:15
  22.0 10.2 %copy-start.6 = (bf16[32,36,128]{2,0,1:T(8,128)(2,1)S(1)}, bf16[32,36,128]{2,0,1:T(8,128)(2,1)}, u32[]{:S(2)}) copy-start(bf16[32,36,128]{2,0,1:T(8,128)(2,1)} %param.15) | copy-start | bytes 884740
  32.2 5.5 %copy-start.3 = (bf16[32,6,12,128]{3,0,2,1:T(8,128)(2,1)S(1)}, bf16[32,6,12,128]{3,0,2,1:T(8,128)(2,1)}, u32[]{:S(2)}) copy-start(bf16[32,6,12,128]{3,0,2,1:T(8,128)(2,1)} %param.9) | copy-start | bytes 1769476
  32.2 5.5 %copy-start.4 = (bf16[32,6,12,128]{3,0,2,1:T(8,128)(2,1)S(1)}, bf16[32,6,12,128]{3,0,2,1:T(8,128)(2,1)}, u32[]{:S(2)}) copy-start(bf16[32,6,12,128]{3,0,2,1:T(8,128)(2,1)} %param.12) | copy-start | bytes 1769476
  43.9 43.1 %all-to-all-start.1 = ((bf16[8,12,48,128]{3,0,1,2:T(8,128)(2,1)}), bf16[8,12,48,128]{3,0,1,2:T(8,128)(2,1)}, u32[]{:S(2)}, u32[]{:S(2)}) async-start(bf16[8,12,48,128]{3,0,1,2:T(8,128)(2,1)} %copy.51), calls=%async_computation.1 | async-start | bytes 2359296 | tf_op jit(solution)/shard_map/all_to_all | solution.py:50
  48.4 20.0 %copy-start.7 = (f32[6]{0:T(128)S(1)}, f32[6]{0:T(128)}, u32[]{:S(2)}) copy-start(f32[6]{0:T(128)} %param.17) | copy-start | bytes 76
  87.1 2.0 %copy-start.2 = (f32[32,2,6,12,128]{4,0,3,2,1:T(8,128)S(1)}, f32[32,2,6,12,128]{4,0,3,2,1:T(8,128)}, u32[]{:S(2)}) copy-start(f32[32,2,6,12,128]{4,0,3,2,1:T(8,128)} %copy.56) | copy-start | bytes 7077892
  93.8 1.3 copy-start.5
  93.8 47.8 %copy-start.1 = (bf16[288,288]{1,0:T(8,128)(2,1)S(1)}, bf16[288,288]{1,0:T(8,128)(2,1)}, u32[]{:S(2)}) copy-start(bf16[288,288]{1,0:T(8,128)(2,1)} %param.16) | copy-start | bytes 497668
